TPU v7x, 128 devices: a whole 4x4x4 slice. The times are simulated.
128 devices in a mesh: freq: 8 (over y_hi, z), src: 16 (over y_lo, x, core).
Axes of the slice: x: 4, y: 4 (y_hi: 2, y_lo: 2; y = y_hi * 2 + y_lo), z: 4, core: 2. Of those that a mesh axis runs over, the one named last changes fastest.
Arguments:
- reflection: bfloat16 [2, 128, 2048, 2048], P(None, 'freq', None, 'src'), may hold values from -0.125 to 0.125
- direct_wave: float32 [2048, 128, 128], P('src', 'freq'), may hold values from -6 to 6
- first_arrival: int32 [2048, 64], P(('src', 'freq')), may hold values from 64 to 191
Outputs:
- focus_minus: float32 [2048, 128, 128], P('src', 'freq')
- focus_plus: float32 [2048, 128, 128], P('src', 'freq')
All inputs are finite; a program needn't handle non-finite values.
Results may differ from a plain program's by a relative error of at most 0.035.
Values may be sent and summed in bfloat16 or wider, within the bound.
A program may use at most 128 MiB of HBM per device.

v0:
```python
import math
import jax
import jax.numpy as jnp
from jax import lax
from jax.sharding import PartitionSpec as P

NT = 512
ITERS = 2


def transform_tables(nfreq, ntime):
    freqs = jnp.arange(1, nfreq + 1, dtype=jnp.int32)
    times = jnp.arange(ntime, dtype=jnp.int32)
    phase = (freqs[:, None] * times[None, :] % ntime).astype(jnp.float32) * (2.0 * math.pi / ntime)
    cosine = jnp.cos(phase)
    sine = jnp.sin(phase)
    inverse = jnp.stack([cosine * (2.0 / ntime), -sine * (2.0 / ntime)]).astype(jnp.bfloat16)
    forward = jnp.stack([cosine, -sine]).astype(jnp.bfloat16)
    return (inverse, forward)


def apply_window(spectrum, first_arrival, inverse, forward):
    rows_count, nfreq, width = spectrum.shape
    half = width // 2
    ntime = inverse.shape[2]
    split = spectrum.reshape(rows_count, nfreq, 2, half)
    signal = jnp.einsum("rfpc,pft->rct", split, inverse, preferred_element_type=jnp.float32)
    times = jnp.arange(ntime, dtype=jnp.int32)
    limit = first_arrival[:, :, None]
    keep = (times[None, None, :] < limit) | (times[None, None, :] > ntime - limit)
    windowed = jnp.where(keep, signal, jnp.zeros_like(signal)).astype(jnp.bfloat16)
    back = jnp.einsum("rct,pft->rfpc", windowed, forward, preferred_element_type=jnp.float32)
    return back.reshape(rows_count, nfreq, width)


def stacked_parts(vectors, factor):
    rounded = vectors.astype(jnp.bfloat16)
    half = rounded.shape[-1] // 2
    swapped = jnp.concatenate([-rounded[..., half:], rounded[..., :half]], axis=-1)
    if factor < 0:
        swapped = -swapped
    return jnp.stack([rounded, swapped])


def to_owners(reflection, vectors, factor):
    operand = stacked_parts(vectors, factor)
    summed = lax.psum_scatter(
        jnp.einsum(
            "pfrs,psfk->rfk", reflection, operand, preferred_element_type=jnp.float32
        ).astype(jnp.bfloat16),
        "src",
        scatter_dimension=0,
        tiled=True,
    )
    return lax.all_to_all(summed, "freq", split_axis=0, concat_axis=1, tiled=True)


def to_groups(spectrum):
    return lax.all_to_all(
        spectrum.astype(jnp.bfloat16), "freq", split_axis=1, concat_axis=0, tiled=True
    ).astype(spectrum.dtype)


def local(reflection, direct_wave, first_arrival):
    nfreq = direct_wave.shape[1] * lax.axis_size("freq")
    inverse, forward = transform_tables(nfreq, NT)
    focus_plus = direct_wave
    focus_minus = direct_wave
    for iteration in range(ITERS):
        spectrum = to_owners(reflection, focus_plus, 1.0)
        focus_minus = to_groups(apply_window(spectrum, first_arrival, inverse, forward))
        spectrum = to_owners(reflection, focus_minus, -1.0)
        update = to_groups(apply_window(spectrum, first_arrival, inverse, forward))
        focus_plus = direct_wave + update
    return (focus_minus, focus_plus)


def solution(mesh):
    in_specs = (P(None, "freq", None, "src"), P("src", "freq", None), P(("src", "freq"), None))
    out_specs = (P("src", "freq", None), P("src", "freq", None))
    return jax.shard_map(local, mesh=mesh, in_specs=in_specs, out_specs=out_specs, check_vma=False)
```

profile of v0, /device:TPU:0, one launch (start us, length us, event | category | flops | bytes accessed | tf_op | source)
XLA Modules:
  0.0 548.1 jit_solution(8581948061272657369)
XLA Ops:
  7.2 1.6 copy.115
  9.1 11.0 %bitcast_convert_fusion.3 = bf16[16,128,2048]{2,1,0:T(8,128)(2,1)} fusion(bf16[2,16,2048,128]{3,2,1,0:T(8,128)(2,1)} %param.3, bf16[1,128,16,128]{1,3,0,2:T(8,128)(2,1)S(1)} %maximum_bitcast_fusion, bf16[1,128,16,128]{1,3,0,2:T(8,128)(2,1)S(1)} %convert_bitcast_fusion.2), kind=kOutput, calls=%fused_computation.3 | convolution fusion | flops 2152202240 | bytes 26214400 | tf_op jit(solution)/shard_map/pfrs,psfk->rfk/dot_general | solution.py:48
  20.1 12.3 %copy.159 = bf16[2048,2048]{1,0:T(8,128)(2,1)} copy(bf16[2048,2048]{0,1:T(8,128)(2,1)} %bitcast.177) | data formatting | bytes 16777216
  32.4 77.2 %reduce-scatter.13.cloned.1.call-done = bf16[128,2048]{1,0:T(8,128)(2,1)} async-done(((bf16[2048,2048]{1,0:T(8,128)(2,1)}), bf16[128,2048]{1,0:T(8,128)(2,1)}) %reduce-scatter.13.cloned.1.call-update) | async-done | bytes 524304
  109.6 1.3 copy.160
  110.9 1.2 copy.96
  112.1 6.6 %all-to-all-start = ((bf16[128,16,128]{2,1,0:T(8,128)(2,1)}), bf16[128,16,128]{2,1,0:T(8,128)(2,1)S(1)}, u32[]{:S(2)}, u32[]{:S(2)}) async-start(bf16[128,16,128]{2,1,0:T(8,128)(2,1)} %copy.96), calls=%async_computation | async-start | bytes 1048576 | tf_op jit(solution)/shard_map/all_to_all | solution.py:55
  118.8 1.9 fusion.69
  120.7 7.8 %all-to-all-done = bf16[128,16,128]{2,1,0:T(8,128)(2,1)S(1)} async-done(((bf16[128,16,128]{2,1,0:T(8,128)(2,1)}), bf16[128,16,128]{2,1,0:T(8,128)(2,1)S(1)}, u32[]{:S(2)}, u32[]{:S(2)}) %all-to-all-start) | async-done | bytes 524320 | tf_op jit(solution)/shard_map/all_to_all | solution.py:55
  128.6 0.4 reshape.255
  129.0 1.8 fusion.25
  130.9 0.4 copy.100
  131.3 13.1 %all_to_all.114 = bf16[16,128,128]{2,0,1:T(8,128)(2,1)S(1)} all-to-all(bf16[16,128,128]{2,0,1:T(8,128)(2,1)S(1)} %copy.100), channel_id=1, replica_groups=mesh['freq'=8,'src'=16] {'freq'}, dimensions={1} | all-to-all | bytes 1048576 | tf_op jit(solution)/shard_map/all_to_all | solution.py:59
  144.4 0.1 copy.102
  144.5 0.5 copy.106
  145.0 0.2 fusion.79
  145.2 0.5 copy.167
  145.7 0.5 copy.168
  146.2 0.1 maximum_negate_fusion
  146.3 11.0 %bitcast_convert_fusion.2 = bf16[16,128,2048]{2,1,0:T(8,128)(2,1)} fusion(bf16[2,16,2048,128]{3,2,1,0:T(8,128)(2,1)} %param.3, bf16[1,128,16,128]{1,3,0,2:T(8,128)(2,1)S(1)} %maximum_negate_fusion, bf16[1,128,16,128]{1,3,0,2:T(8,128)(2,1)S(1)} %copy.106), kind=kOutput, calls=%fused_computation.2 | convolution fusion | flops 2152202240 | bytes 26214400 | tf_op jit(solution)/shard_map/pfrs,psfk->rfk/dot_general | solution.py:48
  157.3 12.3 %copy.161 = bf16[2048,2048]{1,0:T(8,128)(2,1)} copy(bf16[2048,2048]{0,1:T(8,128)(2,1)} %bitcast.178) | data formatting | bytes 16777216
  169.7 71.8 %reduce-scatter.15.cloned.1.call-done = bf16[128,2048]{1,0:T(8,128)(2,1)} async-done(((bf16[2048,2048]{1,0:T(8,128)(2,1)}), bf16[128,2048]{1,0:T(8,128)(2,1)}) %reduce-scatter.15.cloned.1.call-update) | async-done | bytes 524304
  241.4 1.3 copy.162
  242.7 0.4 copy.108
  243.2 16.5 %all_to_all.115 = bf16[128,16,128]{2,1,0:T(8,128)(2,1)S(1)} all-to-all(bf16[128,16,128]{2,1,0:T(8,128)(2,1)S(1)} %copy.108), channel_id=1, replica_groups=mesh['freq'=8,'src'=16] {'freq'}, dimensions={0} | all-to-all | bytes 1048576 | tf_op jit(solution)/shard_map/all_to_all | solution.py:55
  259.7 0.4 reshape.256
  260.1 1.8 fusion.26
  262.0 0.4 copy.112
  262.4 12.7 %all_to_all.116 = bf16[16,128,128]{2,0,1:T(8,128)(2,1)S(1)} all-to-all(bf16[16,128,128]{2,0,1:T(8,128)(2,1)S(1)} %copy.112), channel_id=1, replica_groups=mesh['freq'=8,'src'=16] {'freq'}, dimensions={1} | all-to-all | bytes 1048576 | tf_op jit(solution)/shard_map/all_to_all | solution.py:59
  275.2 0.1 copy.113
  275.4 1.1 copy.114
  276.5 1.6 copy.116
  278.1 0.1 add_convert_fusion
  278.3 11.0 %bitcast_convert_fusion.1 = bf16[16,128,2048]{2,1,0:T(8,128)(2,1)} fusion(bf16[2,16,2048,128]{3,2,1,0:T(8,128)(2,1)} %param.3, bf16[1,128,16,128]{1,3,0,2:T(8,128)(2,1)S(1)} %maximum_bitcast_fusion.1, bf16[1,128,16,128]{1,3,0,2:T(8,128)(2,1)S(1)} %bitcast.185), kind=kOutput, calls=%fused_computation.1 | convolution fusion | flops 2152202240 | bytes 26214400 | tf_op jit(solution)/shard_map/pfrs,psfk->rfk/dot_general | solution.py:48
  289.3 12.3 %copy.163 = bf16[2048,2048]{1,0:T(8,128)(2,1)} copy(bf16[2048,2048]{0,1:T(8,128)(2,1)} %bitcast.179) | data formatting | bytes 16777216
  301.7 71.6 %reduce-scatter.17.cloned.1.call-done = bf16[128,2048]{1,0:T(8,128)(2,1)} async-done(((bf16[2048,2048]{1,0:T(8,128)(2,1)}), bf16[128,2048]{1,0:T(8,128)(2,1)}) %reduce-scatter.17.cloned.1.call-update) | async-done | bytes 524304
  373.3 1.3 copy.164
  374.6 0.4 copy.119
  375.1 16.6 %all_to_all.117 = bf16[128,16,128]{2,1,0:T(8,128)(2,1)S(1)} all-to-all(bf16[128,16,128]{2,1,0:T(8,128)(2,1)S(1)} %copy.119), channel_id=1, replica_groups=mesh['freq'=8,'src'=16] {'freq'}, dimensions={0} | all-to-all | bytes 1048576 | tf_op jit(solution)/shard_map/all_to_all | solution.py:55
  391.8 0.4 reshape.257
  392.2 0.9 fusion.27
  393.2 0.4 copy.123
  393.6 12.7 %all_to_all.118 = bf16[16,128,128]{2,0,1:T(8,128)(2,1)S(1)} all-to-all(bf16[16,128,128]{2,0,1:T(8,128)(2,1)S(1)} %copy.123), channel_id=1, replica_groups=mesh['freq'=8,'src'=16] {'freq'}, dimensions={1} | all-to-all | bytes 1048576 | tf_op jit(solution)/shard_map/all_to_all | solution.py:59
  406.3 0.1 copy.125
  406.5 0.5 copy.129
  406.9 0.2 fusion.78
  407.2 0.5 copy.169
  407.7 0.5 copy.170
  408.1 0.1 maximum_negate_fusion.1
  408.3 11.0 %bitcast_convert_fusion = bf16[16,128,2048]{2,1,0:T(8,128)(2,1)} fusion(bf16[2,16,2048,128]{3,2,1,0:T(8,128)(2,1)} %param.3, bf16[1,128,16,128]{1,3,0,2:T(8,128)(2,1)S(1)} %maximum_negate_fusion.1, bf16[1,128,16,128]{1,3,0,2:T(8,128)(2,1)S(1)} %copy.129), kind=kOutput, calls=%fused_computation | convolution fusion | flops 2152202240 | bytes 26214400 | tf_op jit(solution)/shard_map/pfrs,psfk->rfk/dot_general | solution.py:48
  419.3 12.3 %copy.165 = bf16[2048,2048]{1,0:T(8,128)(2,1)} copy(bf16[2048,2048]{0,1:T(8,128)(2,1)} %bitcast.180) | data formatting | bytes 16777216
  431.6 71.6 %reduce-scatter.19.cloned.1.call-done = bf16[128,2048]{1,0:T(8,128)(2,1)} async-done(((bf16[2048,2048]{1,0:T(8,128)(2,1)}), bf16[128,2048]{1,0:T(8,128)(2,1)}) %reduce-scatter.19.cloned.1.call-update) | async-done | bytes 524304
  503.2 1.3 copy.166
  504.5 0.4 copy.131
  505.0 16.5 %all_to_all.119 = bf16[128,16,128]{2,1,0:T(8,128)(2,1)S(1)} all-to-all(bf16[128,16,128]{2,1,0:T(8,128)(2,1)S(1)} %copy.131), channel_id=1, replica_groups=mesh['freq'=8,'src'=16] {'freq'}, dimensions={0} | all-to-all | bytes 1048576 | tf_op jit(solution)/shard_map/all_to_all | solution.py:55
  521.5 0.4 reshape.258
  521.9 2.6 fusion.28
  524.6 1.1 copy.134
  525.6 1.2 copy.135
  526.8 3.5 all-to-all-start.7
  530.3 1.1 bitcast_convert_fusion.4
  531.4 8.6 %all-to-all-done.7 = bf16[16,128,128]{2,0,1:T(8,128)(2,1)S(1)} async-done(((bf16[16,128,128]{2,0,1:T(8,128)(2,1)}), bf16[16,128,128]{2,0,1:T(8,128)(2,1)S(1)}, u32[]{:S(2)}, u32[]{:S(2)}) %all-to-all-start.7) | async-done | bytes 524320 | tf_op jit(solution)/shard_map/all_to_all | solution.py:59
  540.1 0.1 copy.136
  540.4 1.1 bitcast_add_fusion
  (34 shorter events, 1.3 us)
Async XLA Ops:
  7.2 102.5 %reduce-scatter.13.cloned.1.call-start = ((), (), s32[]{:S(2)}) async-start(), calls=%async_computation.12 | async-start | bytes 8912896
  32.4 86.4 %copy-start.2 = (s32[16,64]{1,0:T(8,128)S(1)}, s32[16,64]{1,0:T(8,128)}, u32[]{:S(2)}) copy-start(s32[16,64]{1,0:T(8,128)} %param.5) | copy-start | bytes 12292
  112.1 16.4 %all-to-all-start = ((bf16[128,16,128]{2,1,0:T(8,128)(2,1)}), bf16[128,16,128]{2,1,0:T(8,128)(2,1)S(1)}, u32[]{:S(2)}, u32[]{:S(2)}) async-start(bf16[128,16,128]{2,1,0:T(8,128)(2,1)} %copy.96), calls=%async_computation | async-start | bytes 1048576 | tf_op jit(solution)/shard_map/all_to_all | solution.py:55
  118.7 122.7 %reduce-scatter.15.cloned.1.call-start = ((), (), s32[]{:S(2)}) async-start(), calls=%async_computation.13 | async-start | bytes 8912896
  169.6 203.7 %reduce-scatter.17.cloned.1.call-start = ((), (), s32[]{:S(2)}) async-start(), calls=%async_computation.14 | async-start | bytes 8912896
  301.6 90.6 %copy-start.1 = (bf16[1,128,512]{2,1,0:T(8,128)(2,1)S(1)}, bf16[1,128,512]{2,1,0:T(8,128)(2,1)}, u32[]{:S(2)}) copy-start(bf16[1,128,512]{2,1,0:T(8,128)(2,1)} %get-tuple-element.15) | copy-start | bytes 393220
  301.6 201.6 %reduce-scatter.19.cloned.1.call-start = ((), (), s32[]{:S(2)}) async-start(), calls=%async_computation.15 | async-start | bytes 8912896
  521.5 18.9 %copy-start = (f32[128,16,128]{2,1,0:T(8,128)S(1)}, f32[128,16,128]{2,1,0:T(8,128)}, u32[]{:S(2)}) copy-start(f32[128,16,128]{2,1,0:T(8,128)} %param.4) | copy-start | bytes 3145732
  526.8 13.2 %all-to-all-start.7 = ((bf16[16,128,128]{2,0,1:T(8,128)(2,1)}), bf16[16,128,128]{2,0,1:T(8,128)(2,1)S(1)}, u32[]{:S(2)}, u32[]{:S(2)}) async-start(bf16[16,128,128]{2,0,1:T(8,128)(2,1)} %copy.135), calls=%async_computation.7 | async-start | bytes 1048576 | tf_op jit(solution)/shard_map/all_to_all | solution.py:59
Sparse Core Ops, SparseCore 0:
  32.5 77.0 reduce-scatter.12
  169.7 71.6 reduce-scatter.14
  301.7 71.5 reduce-scatter.16
  431.7 71.4 reduce-scatter.18
where the time goes:
time: 550 us; the launch traced here: 548 us
  waiting for transfers between devices  309 us (56%)
  blocking collectives  88.1 us (16%)
  local copies, waits for them, and re-layouts  70.4 us (13%)
  matrix products  51.2 us (9%)
  between operations  14.2 us (3%)
  starting transfers between devices  10.3 us (2%)
    unnamed x8, waiting for transfers between devices  292 us
    unnamed x19, local copies, waits for them, and re-layouts  57.8 us
    all_to_all x3, blocking collectives, to_owners(): lax.all_to_all(summed, 'freq', split_axis=0, concat_axis=1, tiled=True)  49.6 us
    dot_general x4, matrix products, to_owners(): jnp.einsum('pfrs,psfk->rfk', reflection, operand, preferred_element_type=...  44 us
    all_to_all x3, blocking collectives, to_groups(): lax.all_to_all(spectrum.astype(jnp.bfloat16), 'freq', split_axis=1, conca...  38.5 us
  transfers between devices with their start and end apart: 6, of which 6 were waited for; matrix products, arithmetic and copies ran while one was open for 1% of the time, Pallas kernels for 0%

commit v1 on v0

--- a/solution.py
+++ b/solution.py
@@ -3,6 +3,7 @@
 import jax.numpy as jnp
 from jax import lax
 from jax.sharding import PartitionSpec as P
+from jax.lax import all_to_all, axis_size
 
 NT = 512
 ITERS = 2
@@ -52,7 +53,15 @@
         scatter_dimension=0,
         tiled=True,
     )
-    return lax.all_to_all(summed, "freq", split_axis=0, concat_axis=1, tiled=True)
+    return jnp.concatenate(
+        all_to_all(
+            jnp.stack(jnp.split(summed, axis_size("freq"), 0), 0),
+            concat_axis=0,
+            split_axis=0,
+            axis_name="freq",
+        ),
+        1,
+    )
 
 
 def to_groups(spectrum):

time: 550 us -> 589 us (1.071)
  local copies, waits for them, and re-layouts: 70.4 us -> 108 us
    another operation x0 -> x44, local copies, waits for them, and re-layouts: none -> 36.5 us  [the longest x40 34.9 us: to_owners(): jnp.stack(jnp.split(summed, axis_size('freq'), 0), 0)]
    unnamed x19 -> x45, local copies, waits for them, and re-layouts: 57.8 us -> 62.8 us
where the time goes in v1:
time: 589 us; the launch traced here: 587 us
  waiting for transfers between devices  308 us (52%)
  local copies, waits for them, and re-layouts  108 us (18%)
  blocking collectives  88 us (15%)
  matrix products  52.1 us (9%)
  between operations  14.4 us (2%)
  starting transfers between devices  10.5 us (2%)
  other arithmetic  6.25 us (1%)
    unnamed x8, waiting for transfers between devices  292 us
    unnamed x45, local copies, waits for them, and re-layouts  62.8 us
    all_to_all x3, blocking collectives, to_owners(): all_to_all(jnp.stack(jnp.split(summed, axis_size('freq'), 0), 0), concat_...  49.5 us
    dot_general x4, matrix products, to_owners(): jnp.einsum('pfrs,psfk->rfk', reflection, operand, preferred_element_type=...  44 us
    all_to_all x3, blocking collectives, to_groups(): lax.all_to_all(spectrum.astype(jnp.bfloat16), 'freq', split_axis=1, conca...  38.5 us
    another operation x40, local copies, waits for them, and re-layouts, to_owners(): jnp.stack(jnp.split(summed, axis_size('freq'), 0), 0)  34.9 us
  transfers between devices with their start and end apart: 6, of which 6 were waited for; matrix products, arithmetic and copies ran while one was open for 1% of the time, Pallas kernels for 0%

profile of v1, /device:TPU:0, one launch (start us, length us, event | category | flops | bytes accessed | tf_op | source)
XLA Modules:
  0.0 586.6 jit_solution(355744042234223433)
XLA Ops:
  7.2 1.6 copy.182
  9.1 11.0 %bitcast_convert_fusion.3 = bf16[16,128,2048]{2,1,0:T(8,128)(2,1)} fusion(bf16[2,16,2048,128]{3,2,1,0:T(8,128)(2,1)} %param.3, bf16[1,128,16,128]{1,3,0,2:T(8,128)(2,1)S(1)} %maximum_bitcast_fusion, bf16[1,128,16,128]{1,3,0,2:T(8,128)(2,1)S(1)} %convert_bitcast_fusion.2), kind=kOutput, calls=%fused_computation.3 | convolution fusion | flops 2152202240 | bytes 26214400 | tf_op jit(solution)/shard_map/pfrs,psfk->rfk/dot_general | solution.py:49
  20.1 12.4 %copy.240 = bf16[2048,2048]{1,0:T(8,128)(2,1)} copy(bf16[2048,2048]{0,1:T(8,128)(2,1)} %bitcast.233) | data formatting | bytes 16777216
  33.0 76.7 %reduce-scatter.13.cloned.1.call-done = bf16[128,2048]{1,0:T(8,128)(2,1)} async-done(((bf16[2048,2048]{1,0:T(8,128)(2,1)}), bf16[128,2048]{1,0:T(8,128)(2,1)}) %reduce-scatter.13.cloned.1.call-update) | async-done | bytes 524304
  109.7 1.3 copy.241
  111.0 2.7 slice_bitcast_fusion.24
  113.7 1.2 copy.156
  114.9 1.2 copy.155
  116.2 1.2 copy.154
  117.4 1.2 copy.153
  118.6 1.2 copy.152
  120.5 0.6 constant_dynamic-update-slice_fusion.7
  121.2 0.6 constant_dynamic-update-slice_fusion.6
  121.8 0.6 constant_dynamic-update-slice_fusion.5
  123.1 0.6 constant_dynamic-update-slice_fusion.3
  124.3 0.6 constant_dynamic-update-slice_fusion.1
  125.6 6.6 %all-to-all-start = ((bf16[8,16,16,128]{3,2,1,0:T(8,128)(2,1)}), bf16[8,16,16,128]{3,2,1,0:T(8,128)(2,1)S(1)}, u32[]{:S(2)}, u32[]{:S(2)}) async-start(bf16[8,16,16,128]{3,2,1,0:T(8,128)(2,1)} %constant_dynamic-update-slice_fusion), calls=%async_computation | async-start | bytes 1048576 | tf_op jit(solution)/shard_map/all_to_all | solution.py:57
  132.3 2.5 fusion.69
  134.8 7.2 %all-to-all-done = bf16[8,16,16,128]{3,2,1,0:T(8,128)(2,1)S(1)} async-done(((bf16[8,16,16,128]{3,2,1,0:T(8,128)(2,1)}), bf16[8,16,16,128]{3,2,1,0:T(8,128)(2,1)S(1)}, u32[]{:S(2)}, u32[]{:S(2)}) %all-to-all-start) | async-done | bytes 524320 | tf_op jit(solution)/shard_map/all_to_all | solution.py:57
  142.5 1.8 fusion.25
  144.8 13.1 %all_to_all.74 = bf16[16,128,128]{2,0,1:T(8,128)(2,1)S(1)} all-to-all(bf16[16,128,128]{2,0,1:T(8,128)(2,1)S(1)} %copy.160), channel_id=1, replica_groups=mesh['freq'=8,'src'=16] {'freq'}, dimensions={1} | all-to-all | bytes 1048576 | tf_op jit(solution)/shard_map/all_to_all | solution.py:68
  159.8 11.0 %bitcast_convert_fusion.2 = bf16[16,128,2048]{2,1,0:T(8,128)(2,1)} fusion(bf16[2,16,2048,128]{3,2,1,0:T(8,128)(2,1)} %param.3, bf16[1,128,16,128]{1,3,0,2:T(8,128)(2,1)S(1)} %maximum_negate_fusion, bf16[1,128,16,128]{1,3,0,2:T(8,128)(2,1)S(1)} %copy.166), kind=kOutput, calls=%fused_computation.2 | convolution fusion | flops 2152202240 | bytes 26214400 | tf_op jit(solution)/shard_map/pfrs,psfk->rfk/dot_general | solution.py:49
  170.8 12.4 %copy.242 = bf16[2048,2048]{1,0:T(8,128)(2,1)} copy(bf16[2048,2048]{0,1:T(8,128)(2,1)} %bitcast.234) | data formatting | bytes 16777216
  183.2 71.8 %reduce-scatter.15.cloned.1.call-done = bf16[128,2048]{1,0:T(8,128)(2,1)} async-done(((bf16[2048,2048]{1,0:T(8,128)(2,1)}), bf16[128,2048]{1,0:T(8,128)(2,1)}) %reduce-scatter.15.cloned.1.call-update) | async-done | bytes 524304
  255.0 1.3 copy.243
  256.3 2.7 slice_bitcast_fusion.16
  258.9 1.2 copy.175
  260.2 1.2 copy.174
  261.4 1.2 copy.173
  262.7 1.2 copy.172
  263.9 1.2 copy.171
  265.9 16.5 %all_to_all.75 = bf16[8,16,16,128]{3,2,1,0:T(8,128)(2,1)S(1)} all-to-all(bf16[8,16,16,128]{3,2,1,0:T(8,128)(2,1)S(1)} %constant_dynamic-update-slice_fusion.8), channel_id=1, replica_groups=mesh['freq'=8,'src'=16] {'freq'}, dimensions={0} | all-to-all | bytes 1048576 | tf_op jit(solution)/shard_map/all_to_all | solution.py:57
  282.9 1.8 fusion.26
  285.2 12.7 %all_to_all.76 = bf16[16,128,128]{2,0,1:T(8,128)(2,1)S(1)} all-to-all(bf16[16,128,128]{2,0,1:T(8,128)(2,1)S(1)} %copy.179), channel_id=1, replica_groups=mesh['freq'=8,'src'=16] {'freq'}, dimensions={1} | all-to-all | bytes 1048576 | tf_op jit(solution)/shard_map/all_to_all | solution.py:68
  298.2 1.1 copy.181
  299.3 1.6 copy.183
  301.1 11.0 %bitcast_convert_fusion.1 = bf16[16,128,2048]{2,1,0:T(8,128)(2,1)} fusion(bf16[2,16,2048,128]{3,2,1,0:T(8,128)(2,1)} %param.3, bf16[1,128,16,128]{1,3,0,2:T(8,128)(2,1)S(1)} %maximum_bitcast_fusion.1, bf16[1,128,16,128]{1,3,0,2:T(8,128)(2,1)S(1)} %bitcast.245), kind=kOutput, calls=%fused_computation.1 | convolution fusion | flops 2152202240 | bytes 26214400 | tf_op jit(solution)/shard_map/pfrs,psfk->rfk/dot_general | solution.py:49
  312.1 12.4 %copy.244 = bf16[2048,2048]{1,0:T(8,128)(2,1)} copy(bf16[2048,2048]{0,1:T(8,128)(2,1)} %bitcast.235) | data formatting | bytes 16777216
  324.8 71.5 %reduce-scatter.17.cloned.1.call-done = bf16[128,2048]{1,0:T(8,128)(2,1)} async-done(((bf16[2048,2048]{1,0:T(8,128)(2,1)}), bf16[128,2048]{1,0:T(8,128)(2,1)}) %reduce-scatter.17.cloned.1.call-update) | async-done | bytes 524304
  396.3 1.3 copy.245
  397.6 2.3 slice_bitcast_fusion.8
  399.9 1.2 copy.193
  401.1 1.2 copy.192
  402.4 1.2 copy.191
  404.8 16.5 %all_to_all.77 = bf16[8,16,16,128]{3,2,1,0:T(8,128)(2,1)S(1)} all-to-all(bf16[8,16,16,128]{3,2,1,0:T(8,128)(2,1)S(1)} %constant_dynamic-update-slice_fusion.16), channel_id=1, replica_groups=mesh['freq'=8,'src'=16] {'freq'}, dimensions={0} | all-to-all | bytes 1048576 | tf_op jit(solution)/shard_map/all_to_all | solution.py:57
  421.8 1.8 fusion.27
  424.1 12.7 %all_to_all.78 = bf16[16,128,128]{2,0,1:T(8,128)(2,1)S(1)} all-to-all(bf16[16,128,128]{2,0,1:T(8,128)(2,1)S(1)} %copy.197), channel_id=1, replica_groups=mesh['freq'=8,'src'=16] {'freq'}, dimensions={1} | all-to-all | bytes 1048576 | tf_op jit(solution)/shard_map/all_to_all | solution.py:68
  438.8 11.0 %bitcast_convert_fusion = bf16[16,128,2048]{2,1,0:T(8,128)(2,1)} fusion(bf16[2,16,2048,128]{3,2,1,0:T(8,128)(2,1)} %param.3, bf16[1,128,16,128]{1,3,0,2:T(8,128)(2,1)S(1)} %maximum_negate_fusion.1, bf16[1,128,16,128]{1,3,0,2:T(8,128)(2,1)S(1)} %copy.203), kind=kOutput, calls=%fused_computation | convolution fusion | flops 2152202240 | bytes 26214400 | tf_op jit(solution)/shard_map/pfrs,psfk->rfk/dot_general | solution.py:49
  449.8 12.4 %copy.246 = bf16[2048,2048]{1,0:T(8,128)(2,1)} copy(bf16[2048,2048]{0,1:T(8,128)(2,1)} %bitcast.236) | data formatting | bytes 16777216
  462.2 71.6 %reduce-scatter.19.cloned.1.call-done = bf16[128,2048]{1,0:T(8,128)(2,1)} async-done(((bf16[2048,2048]{1,0:T(8,128)(2,1)}), bf16[128,2048]{1,0:T(8,128)(2,1)}) %reduce-scatter.19.cloned.1.call-update) | async-done | bytes 524304
  533.8 1.3 copy.247
  535.1 2.5 slice_bitcast_fusion
  537.6 1.2 copy.212
  538.8 1.2 copy.211
  540.1 1.2 copy.210
  541.3 1.2 copy.209
  543.5 16.5 %all_to_all.79 = bf16[8,16,16,128]{3,2,1,0:T(8,128)(2,1)S(1)} all-to-all(bf16[8,16,16,128]{3,2,1,0:T(8,128)(2,1)S(1)} %constant_dynamic-update-slice_fusion.24), channel_id=1, replica_groups=mesh['freq'=8,'src'=16] {'freq'}, dimensions={0} | all-to-all | bytes 1048576 | tf_op jit(solution)/shard_map/all_to_all | solution.py:57
  560.5 2.6 fusion.28
  563.1 1.1 copy.215
  564.2 1.2 copy.216
  565.4 3.5 all-to-all-start.7
  568.9 1.1 bitcast_convert_fusion.4
  570.0 8.6 %all-to-all-done.7 = bf16[16,128,128]{2,0,1:T(8,128)(2,1)S(1)} async-done(((bf16[16,128,128]{2,0,1:T(8,128)(2,1)}), bf16[16,128,128]{2,0,1:T(8,128)(2,1)S(1)}, u32[]{:S(2)}, u32[]{:S(2)}) %all-to-all-start.7) | async-done | bytes 524320 | tf_op jit(solution)/shard_map/all_to_all | solution.py:68
  579.0 1.1 bitcast_add_fusion
  (96 shorter events, 14.3 us)
Async XLA Ops:
  7.2 102.5 %reduce-scatter.13.cloned.1.call-start = ((), (), s32[]{:S(2)}) async-start(), calls=%async_computation.12 | async-start | bytes 8912896
  32.5 99.8 %copy-start.1 = (s32[16,64]{1,0:T(8,128)S(1)}, s32[16,64]{1,0:T(8,128)}, u32[]{:S(2)}) copy-start(s32[16,64]{1,0:T(8,128)} %param.5) | copy-start | bytes 12292
  125.6 16.4 %all-to-all-start = ((bf16[8,16,16,128]{3,2,1,0:T(8,128)(2,1)}), bf16[8,16,16,128]{3,2,1,0:T(8,128)(2,1)S(1)}, u32[]{:S(2)}, u32[]{:S(2)}) async-start(bf16[8,16,16,128]{3,2,1,0:T(8,128)(2,1)} %constant_dynamic-update-slice_fusion), calls=%async_computation | async-start | bytes 1048576 | tf_op jit(solution)/shard_map/all_to_all | solution.py:57
  132.2 122.8 %reduce-scatter.15.cloned.1.call-start = ((), (), s32[]{:S(2)}) async-start(), calls=%async_computation.13 | async-start | bytes 8912896
  183.2 213.1 %reduce-scatter.17.cloned.1.call-start = ((), (), s32[]{:S(2)}) async-start(), calls=%async_computation.14 | async-start | bytes 8912896
  324.5 209.3 %reduce-scatter.19.cloned.1.call-start = ((), (), s32[]{:S(2)}) async-start(), calls=%async_computation.15 | async-start | bytes 8912896
  560.0 18.9 %copy-start = (f32[128,16,128]{2,1,0:T(8,128)S(1)}, f32[128,16,128]{2,1,0:T(8,128)}, u32[]{:S(2)}) copy-start(f32[128,16,128]{2,1,0:T(8,128)} %param.4) | copy-start | bytes 3145732
  565.4 13.2 %all-to-all-start.7 = ((bf16[16,128,128]{2,0,1:T(8,128)(2,1)}), bf16[16,128,128]{2,0,1:T(8,128)(2,1)S(1)}, u32[]{:S(2)}, u32[]{:S(2)}) async-start(bf16[16,128,128]{2,0,1:T(8,128)(2,1)} %copy.216), calls=%async_computation.7 | async-start | bytes 1048576 | tf_op jit(solution)/shard_map/all_to_all | solution.py:68
Sparse Core Ops, SparseCore 0:
  32.6 77.0 reduce-scatter.12
  183.3 71.6 reduce-scatter.14
  324.6 71.6 reduce-scatter.16
  462.3 71.4 reduce-scatter.18
